TPU v7x, 32 devices: a whole 2x2x4 slice. The times are simulated.
32 devices in a mesh: dp: 4 (over y, x), fsdp: 2 (over core), ctx: 4 (over z).
Axes of the slice: x: 2, y: 2, z: 4, core: 2. Of those that a mesh axis runs over, the one named last changes fastest.
Arguments:
- tokens: bfloat16 [16384, 8192], P(('dp', 'ctx')), may hold values from -6 to 6
- grad_hidden: bfloat16 [16384, 256], P(('dp', 'ctx'), 'fsdp'), may hold values from -0.0625 to 0.0625
- master: float32 [256, 8192], P(('fsdp', 'ctx')), may hold values from -3 to 3
- first_moment: float32 [256, 8192], P(('fsdp', 'ctx')), may hold values from -2 to 2
- second_moment: float32 [256, 8192], P(('fsdp', 'ctx')), may hold values from 0.01 to 1
- clip_scale: float32 [], replicated, may hold values from 0.2 to 1
Outputs:
- new_weights: bfloat16 [256, 8192], P('fsdp')
- new_master: float32 [256, 8192], P(('fsdp', 'ctx'))
- new_first: float32 [256, 8192], P(('fsdp', 'ctx'))
- new_second: float32 [256, 8192], P(('fsdp', 'ctx'))
All inputs are finite; a program needn't handle non-finite values.
Results may differ from a plain program's by a relative error of at most 0.005.
Values may be sent and summed in bfloat16 or wider, within the bound.
A program may use at most 128 MiB of HBM per device.

v0:
```python
import jax
import jax.numpy as jnp
from jax import lax
from jax.sharding import PartitionSpec as P

STEP = 10
BETA_ONE = 0.9
BETA_TWO = 0.95
EPSILON = 1e-08
LEARNING_RATE = 0.02
DECAY = 0.1


def contract(columns, tokens):
    return lax.dot_general(
        columns, tokens, (((0,), (0,)), ((), ())), preferred_element_type=jnp.float32
    )


def adamw(grad_sum, master, first_moment, second_moment, clip_scale):
    scaled = clip_scale * grad_sum
    first_new = BETA_ONE * first_moment + (1.0 - BETA_ONE) * scaled
    second_new = BETA_TWO * second_moment + (1.0 - BETA_TWO) * scaled * scaled
    first_hat = first_new / (1.0 - BETA_ONE**STEP)
    second_hat = second_new / (1.0 - BETA_TWO**STEP)
    update = first_hat / (jnp.sqrt(second_hat) + EPSILON)
    fresh_master = master - LEARNING_RATE * (update + DECAY * master)
    return (fresh_master, first_new, second_new)


def per_device(tokens, grad_hidden, master, first_moment, second_moment, clip_scale):
    ctx_count = lax.axis_size("ctx")
    dp_count = lax.axis_size("dp")
    row_dev = master.shape[0]
    width = tokens.shape[1]
    piece_rows = row_dev // dp_count
    tok_rows = grad_hidden.shape[0]
    reordered = (
        grad_hidden.reshape(tok_rows, ctx_count, dp_count, piece_rows)
        .transpose(0, 2, 1, 3)
        .reshape(tok_rows, ctx_count * dp_count * piece_rows)
    )
    partial_terms = contract(reordered, tokens).astype(jnp.bfloat16)
    piece_terms = partial_terms.reshape(dp_count * ctx_count, piece_rows, width)
    received = lax.all_to_all(piece_terms, ("dp", "ctx"), split_axis=0, concat_axis=0, tiled=True)
    piece_grad = jnp.sum(received, axis=0, dtype=jnp.float32)
    offset = lax.axis_index("dp") * piece_rows
    master_piece = lax.dynamic_slice_in_dim(master, offset, piece_rows, 0)
    first_piece = lax.dynamic_slice_in_dim(first_moment, offset, piece_rows, 0)
    second_piece = lax.dynamic_slice_in_dim(second_moment, offset, piece_rows, 0)
    fresh_piece, first_fresh, second_fresh = adamw(
        piece_grad, master_piece, first_piece, second_piece, clip_scale
    )
    new_master, new_first, new_second = (
        lax.all_gather(fresh_piece.astype(jnp.bfloat16), "dp", axis=0, tiled=True).astype(
            fresh_piece.dtype
        ),
        lax.all_gather(first_fresh.astype(jnp.bfloat16), "dp", axis=0, tiled=True).astype(
            first_fresh.dtype
        ),
        lax.all_gather(second_fresh.astype(jnp.bfloat16), "dp", axis=0, tiled=True).astype(
            second_fresh.dtype
        ),
    )
    new_weights = lax.all_gather(new_master.astype(jnp.bfloat16), "ctx", axis=0, tiled=True)
    return (new_weights, new_master, new_first, new_second)


def solution(mesh):
    in_specs = (
        P(("dp", "ctx"), None),
        P(("dp", "ctx"), "fsdp"),
        P(("fsdp", "ctx"), None),
        P(("fsdp", "ctx"), None),
        P(("fsdp", "ctx"), None),
        P(),
    )
    out_specs = (
        P("fsdp", None),
        P(("fsdp", "ctx"), None),
        P(("fsdp", "ctx"), None),
        P(("fsdp", "ctx"), None),
    )
    return jax.shard_map(
        per_device, mesh=mesh, in_specs=in_specs, out_specs=out_specs, check_vma=False
    )
```

profile of v0, /device:TPU:0, one launch (start us, length us, event | category | flops | bytes accessed | tf_op | source)
XLA Modules:
  0.0 141.5 jit_solution(3113973933799284460)
XLA Ops:
  7.2 1.1 copy.10
  8.3 9.5 %fusion = bf16[16,8,8192]{2,1,0:T(8,128)(2,1)} fusion(bf16[1024,128]{0,1:T(8,128)(2,1)S(1)} %bitcast.8, bf16[1024,8192]{1,0:T(8,128)(2,1)} %param.6), kind=kOutput, calls=%fused_computation.1 | convolution fusion | flops 2148532224 | bytes 19136512 | tf_op jit(solution)/shard_map/dot_general | solution.py:15
  17.7 8.3 %all-to-all-start = ((bf16[16,8,8192]{2,1,0:T(8,128)(2,1)}), bf16[16,8,8192]{2,1,0:T(8,128)(2,1)S(1)}, u32[]{:S(2)}, u32[]{:S(2)}) async-start(bf16[16,8,8192]{2,1,0:T(8,128)(2,1)} %fusion), calls=%async_computation | async-start | bytes 4194304 | tf_op jit(solution)/shard_map/all_to_all | solution.py:45
  26.1 0.0 all-gather.2.cloned.1.call-start
  26.8 49.2 %all-to-all-done = bf16[16,8,8192]{2,1,0:T(8,128)(2,1)S(1)} async-done(((bf16[16,8,8192]{2,1,0:T(8,128)(2,1)}), bf16[16,8,8192]{2,1,0:T(8,128)(2,1)S(1)}, u32[]{:S(2)}, u32[]{:S(2)}) %all-to-all-start) | async-done | bytes 2097184 | tf_op jit(solution)/shard_map/all_to_all | solution.py:45
  76.0 0.3 convert_reduce_fusion
  76.3 1.4 fusion.3
  77.7 9.8 %all_gather.12 = bf16[32,8192]{1,0:T(8,128)(2,1)} all-gather(bf16[8,8192]{1,0:T(8,128)(2,1)S(1)} %get-tuple-element.5), channel_id=1, replica_groups=mesh['dp'=4,'fsdp'=2,'ctx'=4] {'dp'}, dimensions={0}, use_global_device_ids=true | all-gather | bytes 655360 | tf_op jit(solution)/shard_map/all_gather | solution.py:55
  87.4 0.0 all-gather.2.cloned.1.call-update
  87.5 2.1 %convert_element_type.28 = f32[32,8192]{1,0:T(8,128)} convert(bf16[32,8192]{1,0:T(8,128)(2,1)} %all_gather.12) | non-fusion elementwise | flops 262144 | bytes 1572864 | tf_op jit(solution)/shard_map/convert_element_type | solution.py:55
  89.5 10.0 %all_gather.15 = bf16[32,8192]{1,0:T(8,128)(2,1)S(1)} all-gather(bf16[8,8192]{1,0:T(8,128)(2,1)S(1)} %get-tuple-element.4), channel_id=1, replica_groups=mesh['dp'=4,'fsdp'=2,'ctx'=4] {'dp'}, dimensions={0}, use_global_device_ids=true | all-gather | bytes 655360 | tf_op jit(solution)/shard_map/all_gather | solution.py:61
  99.5 1.0 convert_element_type.32
  100.6 9.3 %all_gather.14 = bf16[32,8192]{1,0:T(8,128)(2,1)S(1)} all-gather(bf16[8,8192]{1,0:T(8,128)(2,1)S(1)} %get-tuple-element.6), channel_id=1, replica_groups=mesh['dp'=4,'fsdp'=2,'ctx'=4] {'dp'}, dimensions={0}, use_global_device_ids=true | all-gather | bytes 655360 | tf_op jit(solution)/shard_map/all_gather | solution.py:58
  109.9 1.0 convert_element_type.30
  111.0 20.6 %all-gather.2.cloned.1.call-done = bf16[128,8192]{1,0:T(8,128)(2,1)} async-done(((bf16[32,8192]{1,0:T(8,128)(2,1)}), bf16[128,8192]{1,0:T(8,128)(2,1)}) %all-gather.2.cloned.1.call-update) | async-done | bytes 2097168 | tf_op jit(solution)/shard_map/all_gather | solution.py:65
  131.6 3.1 %copy.14 = bf16[128,8192]{1,0:T(8,128)(2,1)} copy(bf16[128,8192]{1,0:T(8,128)(2,1)} %all-gather.2.cloned.1.call-done) | data formatting | bytes 4194304
  (1 shorter events, 0.0 us)
Async XLA Ops:
  17.7 58.3 %all-to-all-start = ((bf16[16,8,8192]{2,1,0:T(8,128)(2,1)}), bf16[16,8,8192]{2,1,0:T(8,128)(2,1)S(1)}, u32[]{:S(2)}, u32[]{:S(2)}) async-start(bf16[16,8,8192]{2,1,0:T(8,128)(2,1)} %fusion), calls=%async_computation | async-start | bytes 4194304 | tf_op jit(solution)/shard_map/all_to_all | solution.py:45
  26.1 105.5 %all-gather.2.cloned.1.call-start = ((), (), s32[]{:S(2)}) async-start(), calls=%async_computation.1 | async-start | bytes 2621440 | tf_op jit(solution)/shard_map/all_gather | solution.py:65
Sparse Core Ops, SparseCore 0:
  87.6 43.9 all-gather.1
where the time goes:
time: 142 us
  waiting for transfers between devices  69.9 us (49%)
  blocking collectives  29.1 us (20%)
  between operations  14.7 us (10%)
  matrix products  9.45 us (7%)
  starting transfers between devices  8.35 us (6%)
  other arithmetic  5.81 us (4%)
  local copies, waits for them, and re-layouts  4.2 us (3%)
    all_to_all x1, waiting for transfers between devices, per_device(): lax.all_to_all(piece_terms, ('dp', 'ctx'), split_axis=0, concat_axis=0, t...  49.2 us
    all_gather x1, waiting for transfers between devices, per_device(): lax.all_gather(new_master.astype(jnp.bfloat16), 'ctx', axis=0, tiled=True)  20.6 us
    all_gather x1, blocking collectives, per_device(): lax.all_gather(second_fresh.astype(jnp.bfloat16), 'dp', axis=0, tiled=True)  10 us
    all_gather x1, blocking collectives, per_device(): lax.all_gather(fresh_piece.astype(jnp.bfloat16), 'dp', axis=0, tiled=True)  9.78 us
    dot_general x1, matrix products, contract(): lax.dot_general(columns, tokens, (((0,), (0,)), ((), ())), preferred_elem...  9.45 us
    all_gather x1, blocking collectives, per_device(): lax.all_gather(first_fresh.astype(jnp.bfloat16), 'dp', axis=0, tiled=True)  9.32 us
    all_to_all x1, starting transfers between devices, per_device(): lax.all_to_all(piece_terms, ('dp', 'ctx'), split_axis=0, concat_axis=0, t...  8.31 us
    unnamed x2, local copies, waits for them, and re-layouts  4.18 us
  transfers between devices with their start and end apart: 2, of which 2 were waited for; matrix products, arithmetic and copies ran while one was open for 3% of the time, Pallas kernels for 0%

commit v1 on v0

--- a/solution.py
+++ b/solution.py
@@ -9,6 +9,18 @@
 EPSILON = 1e-08
 LEARNING_RATE = 0.02
 DECAY = 0.1
+
+
+def doubled_up(array, axis, dim):
+    ways, here = (lax.axis_size(axis), lax.axis_index(axis))
+    grown, reach = (array, 1)
+    while reach < ways:
+        theirs = lax.ppermute(grown, axis, [(d, d ^ reach) for d in range(ways)])
+        mine_first = jnp.concatenate([grown, theirs], axis=dim)
+        theirs_first = jnp.concatenate([theirs, grown], axis=dim)
+        grown = jnp.where(here & reach == 0, mine_first, theirs_first)
+        reach = 2 * reach
+    return grown
 
 
 def contract(columns, tokens):
@@ -55,9 +67,7 @@
         lax.all_gather(fresh_piece.astype(jnp.bfloat16), "dp", axis=0, tiled=True).astype(
             fresh_piece.dtype
         ),
-        lax.all_gather(first_fresh.astype(jnp.bfloat16), "dp", axis=0, tiled=True).astype(
-            first_fresh.dtype
-        ),
+        doubled_up(first_fresh.astype(jnp.bfloat16), "dp", 0).astype(first_fresh.dtype),
         lax.all_gather(second_fresh.astype(jnp.bfloat16), "dp", axis=0, tiled=True).astype(
             second_fresh.dtype
         ),

time: 142 us -> 142 us (level)
  blocking collectives: 29.1 us -> 19.1 us
  waiting for transfers between devices: 69.9 us -> 76.3 us
  starting transfers between devices: 8.35 us -> 11.8 us
    all_gather x1 -> x0, blocking collectives: 9.32 us -> none  [per_device(): lax.all_gather(first_fresh.astype(jnp.bfloat16), 'dp', axis=0, tiled=True)]
    ppermute x0 -> x2, starting transfers between devices: none -> 3.47 us  [doubled_up(): theirs = lax.ppermute(grown, axis, [(d, d ^ reach) for d in range(ways)])]
    ppermute x0 -> x2, waiting for transfers between devices: none -> 3.3 us  [doubled_up(): theirs = lax.ppermute(grown, axis, [(d, d ^ reach) for d in range(ways)])]
    all_gather x1, waiting for transfers between devices: 20.6 us -> 23.8 us  [per_device(): lax.all_gather(new_master.astype(jnp.bfloat16), 'ctx', axis=0, tiled=True)]
  transfers between devices with their start and end apart: 2 -> 4, of which waited for: 2 -> 3; matrix products, arithmetic and copies ran while one was open for 3% -> 3% of each run, Pallas kernels for 0% -> 0%
where the time goes in v1:
time: 142 us
  waiting for transfers between devices  76.3 us (54%)
  blocking collectives  19.1 us (13%)
  between operations  14.7 us (10%)
  starting transfers between devices  11.8 us (8%)
  matrix products  9.45 us (7%)
  other arithmetic  5.86 us (4%)
  local copies, waits for them, and re-layouts  4.2 us (3%)
    all_to_all x1, waiting for transfers between devices, per_device(): lax.all_to_all(piece_terms, ('dp', 'ctx'), split_axis=0, concat_axis=0, t...  49.2 us
    all_gather x1, waiting for transfers between devices, per_device(): lax.all_gather(new_master.astype(jnp.bfloat16), 'ctx', axis=0, tiled=True)  23.8 us
    all_gather x1, blocking collectives, per_device(): lax.all_gather(fresh_piece.astype(jnp.bfloat16), 'dp', axis=0, tiled=True)  9.79 us
    dot_general x1, matrix products, contract(): lax.dot_general(columns, tokens, (((0,), (0,)), ((), ())), preferred_elem...  9.45 us
    all_gather x1, blocking collectives, per_device(): lax.all_gather(second_fresh.astype(jnp.bfloat16), 'dp', axis=0, tiled=True)  9.35 us
    all_to_all x1, starting transfers between devices, per_device(): lax.all_to_all(piece_terms, ('dp', 'ctx'), split_axis=0, concat_axis=0, t...  8.31 us
    unnamed x2, local copies, waits for them, and re-layouts  4.18 us
    ppermute x2, starting transfers between devices, doubled_up(): theirs = lax.ppermute(grown, axis, [(d, d ^ reach) for d in range(ways)])  3.47 us
  transfers between devices with their start and end apart: 4, of which 3 were waited for; matrix products, arithmetic and copies ran while one was open for 3% of the time, Pallas kernels for 0%

profile of v1, /device:TPU:0, one launch (start us, length us, event | category | flops | bytes accessed | tf_op | source)
XLA Modules:
  0.0 141.5 jit_solution(5367716661081964570)
XLA Ops:
  7.2 1.1 copy.10
  8.3 9.5 %fusion = bf16[16,8,8192]{2,1,0:T(8,128)(2,1)} fusion(bf16[1024,128]{0,1:T(8,128)(2,1)S(1)} %bitcast.8, bf16[1024,8192]{1,0:T(8,128)(2,1)} %param.6), kind=kOutput, calls=%fused_computation.1 | convolution fusion | flops 2148532224 | bytes 19136512 | tf_op jit(solution)/shard_map/dot_general | solution.py:27
  17.7 8.3 %all-to-all-start = ((bf16[16,8,8192]{2,1,0:T(8,128)(2,1)}), bf16[16,8,8192]{2,1,0:T(8,128)(2,1)S(1)}, u32[]{:S(2)}, u32[]{:S(2)}) async-start(bf16[16,8,8192]{2,1,0:T(8,128)(2,1)} %fusion), calls=%async_computation | async-start | bytes 4194304 | tf_op jit(solution)/shard_map/all_to_all | solution.py:57
  26.1 0.0 all-gather.2.cloned.1.call-start
  26.8 49.2 %all-to-all-done = bf16[16,8,8192]{2,1,0:T(8,128)(2,1)S(1)} async-done(((bf16[16,8,8192]{2,1,0:T(8,128)(2,1)}), bf16[16,8,8192]{2,1,0:T(8,128)(2,1)S(1)}, u32[]{:S(2)}, u32[]{:S(2)}) %all-to-all-start) | async-done | bytes 2097184 | tf_op jit(solution)/shard_map/all_to_all | solution.py:57
  76.0 0.3 convert_reduce_fusion
  76.3 1.4 fusion.4
  77.7 9.8 %all_gather.9 = bf16[32,8192]{1,0:T(8,128)(2,1)} all-gather(bf16[8,8192]{1,0:T(8,128)(2,1)S(1)} %get-tuple-element.5), channel_id=1, replica_groups=mesh['dp'=4,'fsdp'=2,'ctx'=4] {'dp'}, dimensions={0}, use_global_device_ids=true | all-gather | bytes 655360 | tf_op jit(solution)/shard_map/all_gather | solution.py:67
  87.4 0.0 all-gather.2.cloned.1.call-update
  87.5 1.7 %collective-permute-start = (bf16[8,8192]{1,0:T(8,128)(2,1)S(1)}, bf16[8,8192]{1,0:T(8,128)(2,1)S(1)}, u32[]{:S(2)}, u32[]{:S(2)}) collective-permute-start(bf16[8,8192]{1,0:T(8,128)(2,1)S(1)} %get-tuple-element.6), channel_id=1, source_target_pairs={{0,8},{8,0},{16,24},{24,16},{1,9},{9,1},{17,25},{25,17},{2,10},{10... | collective-permute-start | bytes 393224 | tf_op jit(solution)/shard_map/ppermute | solution.py:18
  89.2 3.3 %collective-permute-done = bf16[8,8192]{1,0:T(8,128)(2,1)S(1)} collective-permute-done((bf16[8,8192]{1,0:T(8,128)(2,1)S(1)}, bf16[8,8192]{1,0:T(8,128)(2,1)S(1)}, u32[]{:S(2)}, u32[]{:S(2)}) %collective-permute-start) | collective-permute-done | bytes 131104 | tf_op jit(solution)/shard_map/ppermute | solution.py:18
  92.6 1.7 %collective-permute-start.1 = (bf16[16,8192]{1,0:T(8,128)(2,1)S(1)}, bf16[16,8192]{1,0:T(8,128)(2,1)S(1)}, u32[]{:S(2)}, u32[]{:S(2)}) collective-permute-start(bf16[16,8192]{1,0:T(8,128)(2,1)S(1)} %maximum_select_fusion.1), channel_id=1, source_target_pairs={{0,16},{8,24},{16,0},{24,8},{1,17},{9,25},{17,1},{25,9},{2,18},{10... | collective-permute-start | bytes 786440 | tf_op jit(solution)/shard_map/ppermute | solution.py:18
  94.3 2.1 %convert_element_type.28 = f32[32,8192]{1,0:T(8,128)} convert(bf16[32,8192]{1,0:T(8,128)(2,1)} %all_gather.9) | non-fusion elementwise | flops 262144 | bytes 1572864 | tf_op jit(solution)/shard_map/convert_element_type | solution.py:67
  96.4 9.3 %all_gather.11 = bf16[32,8192]{1,0:T(8,128)(2,1)S(1)} all-gather(bf16[8,8192]{1,0:T(8,128)(2,1)S(1)} %get-tuple-element.4), channel_id=1, replica_groups=mesh['dp'=4,'fsdp'=2,'ctx'=4] {'dp'}, dimensions={0}, use_global_device_ids=true | all-gather | bytes 655360 | tf_op jit(solution)/shard_map/all_gather | solution.py:71
  105.7 1.0 convert_element_type.32
  106.8 0.0 collective-permute-done.1
  106.8 1.0 fusion.1
  107.8 23.8 %all-gather.2.cloned.1.call-done = bf16[128,8192]{1,0:T(8,128)(2,1)} async-done(((bf16[32,8192]{1,0:T(8,128)(2,1)}), bf16[128,8192]{1,0:T(8,128)(2,1)}) %all-gather.2.cloned.1.call-update) | async-done | bytes 2097168 | tf_op jit(solution)/shard_map/all_gather | solution.py:75
  131.6 3.1 %copy.14 = bf16[128,8192]{1,0:T(8,128)(2,1)} copy(bf16[128,8192]{1,0:T(8,128)(2,1)} %all-gather.2.cloned.1.call-done) | data formatting | bytes 4194304
  (2 shorter events, 0.1 us)
Async XLA Ops:
  17.7 58.3 %all-to-all-start = ((bf16[16,8,8192]{2,1,0:T(8,128)(2,1)}), bf16[16,8,8192]{2,1,0:T(8,128)(2,1)S(1)}, u32[]{:S(2)}, u32[]{:S(2)}) async-start(bf16[16,8,8192]{2,1,0:T(8,128)(2,1)} %fusion), calls=%async_computation | async-start | bytes 4194304 | tf_op jit(solution)/shard_map/all_to_all | solution.py:57
  26.1 105.5 %all-gather.2.cloned.1.call-start = ((), (), s32[]{:S(2)}) async-start(), calls=%async_computation.1 | async-start | bytes 2621440 | tf_op jit(solution)/shard_map/all_gather | solution.py:75
  87.5 5.0 %collective-permute-start = (bf16[8,8192]{1,0:T(8,128)(2,1)S(1)}, bf16[8,8192]{1,0:T(8,128)(2,1)S(1)}, u32[]{:S(2)}, u32[]{:S(2)}) collective-permute-start(bf16[8,8192]{1,0:T(8,128)(2,1)S(1)} %get-tuple-element.6), channel_id=1, source_target_pairs={{0,8},{8,0},{16,24},{24,16},{1,9},{9,1},{17,25},{25,17},{2,10},{10... | collective-permute-start | bytes 393224 | tf_op jit(solution)/shard_map/ppermute | solution.py:18
  92.6 14.2 %collective-permute-start.1 = (bf16[16,8192]{1,0:T(8,128)(2,1)S(1)}, bf16[16,8192]{1,0:T(8,128)(2,1)S(1)}, u32[]{:S(2)}, u32[]{:S(2)}) collective-permute-start(bf16[16,8192]{1,0:T(8,128)(2,1)S(1)} %maximum_select_fusion.1), channel_id=1, source_target_pairs={{0,16},{8,24},{16,0},{24,8},{1,17},{9,25},{17,1},{25,9},{2,18},{10... | collective-permute-start | bytes 786440 | tf_op jit(solution)/shard_map/ppermute | solution.py:18
Sparse Core Ops, SparseCore 0:
  87.6 43.9 all-gather.1
